TPU v7x, 32 devices: a whole 2x2x4 slice. The times are simulated.
32 devices in a mesh: seqs: 4 (over y, x), row: 2 (over core), col: 4 (over z).
Axes of the slice: x: 2, y: 2, z: 4, core: 2. Of those that a mesh axis runs over, the one named last changes fastest.
Arguments:
- tokens: bfloat16 [32, 768, 1024], P('seqs', 'col', 'row'), may hold values from -6 to 6
- lengths: int32 [32], P('seqs'), may hold values from 256 to 1024, as said below
- query_weight: float32 [768, 768], P('row', 'col'), may hold values from -0.21875 to 0.21875
- query_bias: float32 [768], P('col'), may hold values from -3 to 3
- key_weight: float32 [768, 768], P('row', 'col'), may hold values from -0.21875 to 0.21875
- value_weight: float32 [768, 768], P('row', 'col'), may hold values from -0.21875 to 0.21875
- value_bias: float32 [768], P('col'), may hold values from -0.4375 to 0.4375
- out_weight: float32 [768, 768], P('col', 'row'), may hold values from -4 to 4
- out_bias: float32 [768], P('col'), may hold values from -1.5 to 1.5
- first_gain: float32 [768], P('col'), may hold values from 0.5 to 1.5
- first_shift: float32 [768], P('col'), may hold values from -3 to 3
- up_weight: float32 [768, 3072], P('row', 'col'), may hold values from -0.21875 to 0.21875
- up_bias: float32 [3072], P('col'), may hold values from -3 to 3
- down_weight: float32 [768, 3072], P('row', 'col'), may hold values from -0.109375 to 0.109375
- down_bias: float32 [768], P('col'), may hold values from -3 to 3
- second_gain: float32 [768], P('col'), may hold values from 0.5 to 1.5
- second_shift: float32 [768], P('col'), may hold values from -3 to 3
- cotangent: bfloat16 [32, 768, 1024], P('seqs', 'col', 'row'), may hold values from -6 to 6
Outputs:
- layer_output: bfloat16 [32, 768, 1024], P('seqs', 'col', 'row')
- tokens_grad: bfloat16 [32, 768, 1024], P('seqs', 'col', 'row')
- query_weight_grad: float32 [768, 768], P('row', 'col')
- query_bias_grad: float32 [768], P('col')
- key_weight_grad: float32 [768, 768], P('row', 'col')
- value_weight_grad: float32 [768, 768], P('row', 'col')
- value_bias_grad: float32 [768], P('col')
- out_weight_grad: float32 [768, 768], P('col', 'row')
- out_bias_grad: float32 [768], P('col')
- first_gain_grad: float32 [768], P('col')
- first_shift_grad: float32 [768], P('col')
- up_weight_grad: float32 [768, 3072], P('row', 'col')
- up_bias_grad: float32 [3072], P('col')
- down_weight_grad: float32 [768, 3072], P('row', 'col')
- down_bias_grad: float32 [768], P('col')
- second_gain_grad: float32 [768], P('col')
- second_shift_grad: float32 [768], P('col')
Inputs may be any that keep to these rules, and one draw needn't show every extreme that they name: Sequence s holds live tokens in its first lengths[s] slots and padding after; at least one sequence fills all 1024 slots.
All inputs are finite; a program needn't handle non-finite values.
Results may differ from a plain program's by a relative error of at most 0.018.
Values may be sent and summed in bfloat16 or wider, within the bound.
No kernel may reach another device: no remote copies, remote signals or barrier semaphores. Data moves between devices by JAX's collectives and lax.ppermute only.
A program may use at most 384 MiB of HBM per device.

v0:
```python
from functools import partial
import math

import jax
import jax.numpy as jnp
from jax import lax
from jax.sharding import PartitionSpec as P

HD = 64


epsilon = 1e-05
masked = -1e30


def inner(left_side, right_side):
    return lax.dot_general(
        left_side, right_side, (((0,), (0,)), ((), ())), preferred_element_type=jnp.float32
    )


def against(left_side, right_side):
    return lax.dot_general(
        left_side, right_side, (((1,), (1,)), ((), ())), preferred_element_type=jnp.float32
    )


def spread_cols(local_piece):
    return lax.all_gather(local_piece, "col", axis=1, tiled=True)


def reduce_cols(partial_term):
    return lax.psum_scatter(partial_term, "col", scatter_dimension=1, tiled=True)


def pair_sums(sum_one, sum_two):
    return lax.psum((sum_one, sum_two), "col")


def normalize(hidden, gain_cols, shift_cols, full_width):
    total_sum, square_sum = pair_sums(jnp.sum(hidden, axis=1), jnp.sum(hidden * hidden, axis=1))
    centre = total_sum / full_width
    inverse = lax.rsqrt(square_sum / full_width - centre * centre + epsilon)
    normed = (hidden - centre[:, None]) * inverse[:, None]
    return (normed * gain_cols + shift_cols, normed, inverse)


def norm_back(grad_out, normed, inverse, gain_cols, full_width):
    scaled = grad_out * gain_cols
    sum_scaled, sum_normed = pair_sums(jnp.sum(scaled, axis=1), jnp.sum(scaled * normed, axis=1))
    return inverse[:, None] * (
        scaled - sum_scaled[:, None] / full_width - normed * sum_normed[:, None] / full_width
    )


def split_heads(tensor):
    return tensor.reshape(tensor.shape[0], tensor.shape[1], tensor.shape[2] // HD, HD)


def blocks_of(tensor, per_step):
    return tensor.reshape((tensor.shape[0] // per_step, per_step) + tensor.shape[1:])


def unblock(tensor):
    return tensor.reshape((tensor.shape[0] * tensor.shape[1],) + tensor.shape[2:])


def score_block(query_part, key_part, limits):
    product = jnp.einsum(
        "gqhd,gkhd->ghqk",
        split_heads(query_part),
        split_heads(key_part),
        preferred_element_type=jnp.float32,
    )
    position = jnp.arange(key_part.shape[1], dtype=jnp.int32)
    allowed = position[None, :] < limits[:, None]
    return jnp.where(allowed[:, None, None, :], product * (1.0 / math.sqrt(HD)), masked)


def attend_block(operands):
    query_part, key_part, value_part, limits = operands
    scores = score_block(query_part, key_part, limits)
    peak = jnp.max(scores, axis=3, keepdims=True)
    logsum = peak + jnp.log(jnp.sum(jnp.exp(scores - peak), axis=3, keepdims=True))
    probs_low = jnp.exp(scores - logsum).astype(jnp.bfloat16)
    mixed_heads = jnp.einsum(
        "ghqk,gkhd->gqhd", probs_low, split_heads(value_part), preferred_element_type=jnp.float32
    )
    return (mixed_heads.reshape(query_part.shape).astype(jnp.bfloat16), logsum[..., 0])


def query_block(operands, with_keys):
    query_part, key_part, value_part, limits, logsum, grad_part = operands
    scale = 1.0 / math.sqrt(HD)
    scores = score_block(query_part, key_part, limits)
    probs = jnp.exp(scores - logsum[..., None])
    grad_probs = jnp.einsum(
        "gqhd,gkhd->ghqk",
        split_heads(grad_part),
        split_heads(value_part),
        preferred_element_type=jnp.float32,
    )
    weighted = jnp.sum(probs * grad_probs, axis=3)
    grad_scores = (probs * (grad_probs - weighted[..., None])).astype(jnp.bfloat16)
    grad_query = (
        jnp.einsum(
            "ghqk,gkhd->gqhd",
            grad_scores,
            split_heads(key_part),
            preferred_element_type=jnp.float32,
        )
        * scale
    )
    grad_query = grad_query.reshape(query_part.shape)
    grad_key = (
        jnp.einsum(
            "ghqk,gqhd->gkhd",
            grad_scores,
            split_heads(query_part),
            preferred_element_type=jnp.float32,
        )
        * scale
    )
    grad_value = jnp.einsum(
        "ghqk,gqhd->gkhd",
        probs.astype(jnp.bfloat16),
        split_heads(grad_part),
        preferred_element_type=jnp.float32,
    )
    return (grad_query, grad_key.reshape(key_part.shape), grad_value.reshape(key_part.shape))


def local(
    tokens,
    lengths,
    query_weight,
    query_bias,
    key_weight,
    value_weight,
    value_bias,
    out_weight,
    out_bias,
    first_gain,
    first_shift,
    up_weight,
    up_bias,
    down_weight,
    down_bias,
    second_gain,
    second_shift,
    cotangent,
):
    seq_count, col_width, seq_rows = tokens.shape
    row_count = seq_count * seq_rows
    full_width = col_width * lax.axis_size("col")
    target = max(1, 512 // seq_rows)
    group_size = max(
        [
            member
            for member in range(1, seq_count + 1)
            if seq_count % member == 0 and member <= target
        ]
    )
    shaped = (seq_count, seq_rows, col_width)
    row_start = lax.axis_index("row") * seq_rows
    positions = row_start + jnp.arange(seq_rows, dtype=jnp.int32)
    valid = (positions[None, :] < lengths[:, None]).astype(jnp.float32).reshape(row_count, 1)
    query_full, key_full, value_full, up_full, out_full, down_full = (
        lax.all_gather(query_weight.astype(jnp.bfloat16), "row", axis=0, tiled=True),
        lax.all_gather(key_weight.astype(jnp.bfloat16), "row", axis=0, tiled=True),
        lax.all_gather(value_weight.astype(jnp.bfloat16), "row", axis=0, tiled=True),
        lax.all_gather(up_weight.astype(jnp.bfloat16), "row", axis=0, tiled=True),
        lax.all_gather(out_weight.astype(jnp.bfloat16), "row", axis=1, tiled=True),
        lax.all_gather(down_weight.astype(jnp.bfloat16), "row", axis=0, tiled=True),
    )
    flat_tokens = jnp.transpose(tokens, (0, 2, 1)).reshape(row_count, col_width)
    token_rows = spread_cols(flat_tokens)
    query_low = (
        jnp.dot(token_rows, query_full, preferred_element_type=jnp.float32) + query_bias
    ).astype(jnp.bfloat16)
    key_low = jnp.dot(token_rows, key_full, preferred_element_type=jnp.float32).astype(jnp.bfloat16)
    value_low = (
        jnp.dot(token_rows, value_full, preferred_element_type=jnp.float32) + value_bias
    ).astype(jnp.bfloat16)
    query_seq = query_low.reshape(shaped)
    key_seq = key_low.reshape(shaped)
    value_seq = value_low.reshape(shaped)
    key_rows, value_rows = (
        lax.all_gather(key_seq, "row", axis=1, tiled=True),
        lax.all_gather(value_seq, "row", axis=1, tiled=True),
    )
    head_mixed, logsum = lax.map(
        attend_block,
        (
            blocks_of(query_seq, group_size),
            blocks_of(key_rows, group_size),
            blocks_of(value_rows, group_size),
            blocks_of(lengths, group_size),
        ),
    )
    head_mixed = unblock(head_mixed).reshape(row_count, col_width)
    logsum = unblock(logsum)
    attn_out = (
        reduce_cols(jnp.dot(head_mixed, out_full, preferred_element_type=jnp.float32)) + out_bias
    )
    first_out, first_normed, first_inverse = normalize(
        flat_tokens.astype(jnp.float32) + attn_out, first_gain, first_shift, full_width
    )
    first_rows = spread_cols(first_out.astype(jnp.bfloat16))
    pre_act = jnp.dot(first_rows, up_full, preferred_element_type=jnp.float32) + up_bias
    gelu_out, gelu_back = jax.vjp(partial(jax.nn.gelu, approximate=False), pre_act)
    activated = gelu_out.astype(jnp.bfloat16)
    branch_out = reduce_cols(against(activated, down_full)) + down_bias
    second_out, second_normed, second_inverse = normalize(
        first_out + branch_out, second_gain, second_shift, full_width
    )
    layer_output = jnp.transpose(second_out.astype(jnp.bfloat16).reshape(shaped), (0, 2, 1))
    grad_out = (
        jnp.transpose(cotangent, (0, 2, 1)).reshape(row_count, col_width).astype(jnp.float32)
        * valid
    )
    second_gain_grad = jnp.sum(grad_out * second_normed, axis=0)
    second_shift_grad = jnp.sum(grad_out, axis=0)
    grad_second = norm_back(grad_out, second_normed, second_inverse, second_gain, full_width)
    grad_down = grad_second.astype(jnp.bfloat16)
    down_bias_grad = jnp.sum(grad_down, axis=0, dtype=jnp.float32)
    grad_down_rows = spread_cols(grad_down)
    down_weight_grad = inner(grad_down_rows, activated)
    grad_act = jnp.dot(grad_down_rows, down_full, preferred_element_type=jnp.float32)
    grad_pre = gelu_back(grad_act)[0].astype(jnp.bfloat16)
    up_bias_grad = jnp.sum(grad_pre, axis=0, dtype=jnp.float32)
    up_weight_grad = inner(first_rows, grad_pre)
    grad_first = grad_second + reduce_cols(against(grad_pre, up_full))
    first_gain_grad = jnp.sum(grad_first * first_normed, axis=0)
    first_shift_grad = jnp.sum(grad_first, axis=0)
    grad_resid = norm_back(grad_first, first_normed, first_inverse, first_gain, full_width)
    grad_attn = grad_resid.astype(jnp.bfloat16)
    out_bias_grad = jnp.sum(grad_attn, axis=0, dtype=jnp.float32)
    grad_attn_rows = spread_cols(grad_attn)
    out_weight_grad = inner(head_mixed, grad_attn_rows)
    grad_mixed = against(grad_attn_rows, out_full).astype(jnp.bfloat16).reshape(shaped)
    operands = (
        blocks_of(query_seq, group_size),
        blocks_of(key_rows, group_size),
        blocks_of(value_rows, group_size),
        blocks_of(lengths, group_size),
        blocks_of(logsum, group_size),
        blocks_of(grad_mixed, group_size),
    )
    grad_query, key_terms, value_terms = lax.map(partial(query_block, with_keys=True), operands)
    grad_key, grad_value = (
        lax.psum_scatter(
            unblock(key_terms).astype(jnp.bfloat16), "row", scatter_dimension=1, tiled=True
        ).astype(jnp.float32),
        lax.psum_scatter(
            unblock(value_terms).astype(jnp.bfloat16), "row", scatter_dimension=1, tiled=True
        ).astype(jnp.float32),
    )
    grad_query = unblock(grad_query).reshape(row_count, col_width).astype(jnp.bfloat16)
    grad_key = grad_key.reshape(row_count, col_width).astype(jnp.bfloat16)
    grad_value = grad_value.reshape(row_count, col_width).astype(jnp.bfloat16)
    query_bias_grad = jnp.sum(grad_query, axis=0, dtype=jnp.float32)
    value_bias_grad = jnp.sum(grad_value, axis=0, dtype=jnp.float32)
    query_weight_grad = inner(token_rows, grad_query)
    key_weight_grad = inner(token_rows, grad_key)
    value_weight_grad = inner(token_rows, grad_value)
    token_terms = (
        against(grad_query, query_full)
        + against(grad_key, key_full)
        + against(grad_value, value_full)
    )
    tokens_grad = jnp.transpose(
        (grad_resid + reduce_cols(token_terms)).astype(jnp.bfloat16).reshape(shaped), (0, 2, 1)
    )
    sum_query, sum_key, sum_value, sum_up, sum_out, sum_down = (
        lax.psum_scatter(
            query_weight_grad.astype(jnp.bfloat16), "row", scatter_dimension=0, tiled=True
        ).astype(jnp.float32),
        lax.psum_scatter(
            key_weight_grad.astype(jnp.bfloat16), "row", scatter_dimension=0, tiled=True
        ).astype(jnp.float32),
        lax.psum_scatter(
            value_weight_grad.astype(jnp.bfloat16), "row", scatter_dimension=0, tiled=True
        ).astype(jnp.float32),
        lax.psum_scatter(
            up_weight_grad.astype(jnp.bfloat16), "row", scatter_dimension=0, tiled=True
        ).astype(jnp.float32),
        lax.psum_scatter(
            out_weight_grad.astype(jnp.bfloat16), "row", scatter_dimension=1, tiled=True
        ).astype(jnp.float32),
        lax.psum_scatter(
            down_weight_grad.astype(jnp.bfloat16), "row", scatter_dimension=0, tiled=True
        ).astype(jnp.float32),
    )
    sum_query, sum_key, sum_value, sum_up, sum_out, sum_down = (
        lax.psum(sum_query.astype(jnp.bfloat16), "seqs").astype(jnp.float32),
        lax.psum(sum_key.astype(jnp.bfloat16), "seqs").astype(jnp.float32),
        lax.psum(sum_value.astype(jnp.bfloat16), "seqs").astype(jnp.float32),
        lax.psum(sum_up.astype(jnp.bfloat16), "seqs").astype(jnp.float32),
        lax.psum(sum_out.astype(jnp.bfloat16), "seqs").astype(jnp.float32),
        lax.psum(sum_down.astype(jnp.bfloat16), "seqs").astype(jnp.float32),
    )
    (
        query_bias_grad,
        value_bias_grad,
        out_bias_grad,
        first_gain_grad,
        first_shift_grad,
        up_bias_grad,
        down_bias_grad,
        second_gain_grad,
        second_shift_grad,
    ) = lax.psum(
        (
            query_bias_grad,
            value_bias_grad,
            out_bias_grad,
            first_gain_grad,
            first_shift_grad,
            up_bias_grad,
            down_bias_grad,
            second_gain_grad,
            second_shift_grad,
        ),
        ("seqs", "row"),
    )
    return (
        layer_output,
        tokens_grad,
        sum_query,
        query_bias_grad,
        sum_key,
        sum_value,
        value_bias_grad,
        sum_out,
        out_bias_grad,
        first_gain_grad,
        first_shift_grad,
        sum_up,
        up_bias_grad,
        sum_down,
        down_bias_grad,
        second_gain_grad,
        second_shift_grad,
    )


def solution(mesh):
    in_specs = (
        P("seqs", "col", "row"),
        P("seqs"),
        P("row", "col"),
        P("col"),
        P("row", "col"),
        P("row", "col"),
        P("col"),
        P("col", "row"),
        P("col"),
        P("col"),
        P("col"),
        P("row", "col"),
        P("col"),
        P("row", "col"),
        P("col"),
        P("col"),
        P("col"),
        P("seqs", "col", "row"),
    )
    out_specs = (
        P("seqs", "col", "row"),
        P("seqs", "col", "row"),
        P("row", "col"),
        P("col"),
        P("row", "col"),
        P("row", "col"),
        P("col"),
        P("col", "row"),
        P("col"),
        P("col"),
        P("col"),
        P("row", "col"),
        P("col"),
        P("row", "col"),
        P("col"),
        P("col"),
        P("col"),
    )
    return jax.shard_map(local, mesh=mesh, in_specs=in_specs, out_specs=out_specs, check_vma=False)
```

profile of v0, /device:TPU:0, one launch (start us, length us, event | category | flops | bytes accessed | tf_op | source)
XLA Modules:
  0.0 1891.1 jit_solution(17458216411057374380)
XLA Ops:
  12.3 116.0 %all-gather.9.cloned.1.call-done = bf16[4096,768]{0,1:T(8,128)(2,1)} async-done(((bf16[4096,192]{0,1:T(8,128)(2,1)}), bf16[4096,768]{0,1:T(8,128)(2,1)}) %all-gather.9.cloned.1.call-update) | async-done | bytes 6291472 | tf_op jit(solution)/shard_map/all_gather | solution.py:29
  151.9 7.5 all-gather.13.cloned.1.call-done
  159.4 58.2 %while.26 = (s32[]{:T(128)}, bf16[8,1,512,192]{2,3,1,0:T(8,128)(2,1)S(1)}, f32[8,1,3,512]{3,2,1,0:T(4,128)}, bf16[8,1,1024,192]{2,3,1,0:T(8,128)(2,1)}, s32[8,1]...) while((s32[]{:T(128)}, ...), condition=%wide.region_3.4_spmd, body=%wide.region_0.3_spmd.sunk | while | flops 420052480 | bytes 22469232 | solution.py:192
  219.1 6.4 fusion.38
  227.9 210.8 %reduce-scatter.21.cloned.1.call-done = f32[4096,192]{0,1:T(8,128)} async-done(((f32[4096,768]{0,1:T(8,128)}), f32[4096,192]{0,1:T(8,128)}) %reduce-scatter.21.cloned.1.call-update) | async-done | bytes 3145744 | tf_op jit(solution)/shard_map/reduce_scatter | solution.py:33
  441.8 18.8 all-reduce.4
  464.8 111.6 %all-gather.15.cloned.1.call-done = bf16[4096,768]{0,1:T(8,128)(2,1)} async-done(((bf16[4096,192]{0,1:T(8,128)(2,1)}), bf16[4096,768]{0,1:T(8,128)(2,1)}) %all-gather.15.cloned.1.call-update) | async-done | bytes 6291472 | tf_op jit(solution)/shard_map/all_gather | solution.py:29
  576.3 35.5 %multiply_convert_fusion.1 = (bf16[4096,768]{1,0:T(8,128)(2,1)}, f32[4096,768]{1,0:T(8,128)}, f32[4096,768]{1,0:T(8,128)}) fusion(f32[768]{0:T(1024)S(1)} %copy-done.52, bf16[4096,768]{0,1:T(8,128)(2,1)} %all-gather.15.cloned.1.call-done, bf16[768,768]{1,0:T(8,128)(2,1)} %all-gather.17.cloned.1.call-done), kind=kOutput, calls=%fused_computation.42 | convolution fusion | flops 5039456256 | bytes 38931456 | tf_op jit(solution)/shard_map/dot_general | solution.py:210
  611.8 10.4 fusion.39
  627.5 204.9 %reduce-scatter.23.cloned.1.call-done = f32[4096,192]{0,1:T(8,128)} async-done(((f32[4096,768]{0,1:T(8,128)}), f32[4096,192]{0,1:T(8,128)}) %reduce-scatter.23.cloned.1.call-update) | async-done | bytes 3145744 | tf_op jit(solution)/shard_map/reduce_scatter | solution.py:33
  837.1 19.3 %all-reduce.3 = (f32[4096]{0:T(1024)S(1)}, f32[4096]{0:T(1024)S(1)}) all-reduce(f32[4096]{0:T(1024)S(1)} %get-tuple-element.172, f32[4096]{0:T(1024)S(1)} %get-tuple-element.171), channel_id=1, replica_groups=mesh['seqs'=4,'row'=2,'col'=4] {'col'}, use_global_device_ids=true, to_apply=%region_13.14 | all-reduce | flops 8192 | bytes 65536 | tf_op jit(solution)/shard_map/psum | solution.py:37
  861.0 15.8 all-reduce.2
  876.8 6.2 convert_reduce_fusion.1
  883.1 115.1 %all-gather.21.cloned.1.call-done = bf16[4096,768]{0,1:T(8,128)(2,1)} async-done(((bf16[4096,192]{0,1:T(8,128)(2,1)}), bf16[4096,768]{0,1:T(8,128)(2,1)}) %all-gather.21.cloned.1.call-update) | async-done | bytes 6291472 | tf_op jit(solution)/shard_map/all_gather | solution.py:29
  998.1 19.8 %convert_reduce_fusion = (f32[768]{0:T(1024)}, bf16[4096,768]{1,0:T(8,128)(2,1)}) fusion(f32[4096,768]{1,0:T(8,128)} %get-tuple-element.245, f32[4096,768]{1,0:T(8,128)} %get-tuple-element.262, f32[768]{0:T(1024)S(1)} %copy-done.52, bf16[4096,768]{0,1:T(8,128)(2,1)} %all-gather.21.cloned.1.call-done, bf16[768,768]{1,0:T(8,128)(2,1)} %all-gather.19.cloned.1.call-done), kind=kOutput, calls=%fused_computation.39 | convolution fusion | flops 4885314560 | bytes 38934528 | tf_op jit(solution)/shard_map/dot_general | solution.py:229
  1017.9 10.7 fusion.40
  1028.9 210.0 %reduce-scatter.25.cloned.1.call-done = f32[4096,192]{0,1:T(8,128)} async-done(((f32[4096,768]{0,1:T(8,128)}), f32[4096,192]{0,1:T(8,128)}) %reduce-scatter.25.cloned.1.call-update) | async-done | bytes 3145744 | tf_op jit(solution)/shard_map/reduce_scatter | solution.py:33
  1238.9 7.6 multiply_reduce_fusion.2
  1246.5 18.8 all-reduce.1
  1269.9 113.8 %all-gather.23.cloned.1.call-done = bf16[4096,768]{0,1:T(8,128)(2,1)} async-done(((bf16[4096,192]{0,1:T(8,128)(2,1)}), bf16[4096,768]{0,1:T(8,128)(2,1)}) %all-gather.23.cloned.1.call-update) | async-done | bytes 6291472 | tf_op jit(solution)/shard_map/all_gather | solution.py:29
  1389.0 111.8 %while.27 = (s32[]{:T(128)}, bf16[8,1,512,192]{2,3,1,0:T(8,128)(2,1)S(1)}, bf16[8,1,1024,192]{2,3,1,0:T(8,128)(2,1)}, bf16[8,1,1024,192]{2,3,1,0:T(8,128)(2,1)},...) while((s32[]{:T(128)}, ...), condition=%wide.region_25.26_spmd, body=%wide.region_23.25_spmd.sunk | while | flops 1030815232 | bytes 54508180 | solution.py:250
  1518.9 5.9 fusion.25
  1534.5 9.8 convolution_convert_fusion.2
  1544.4 9.9 convolution_convert_fusion.3
  1554.7 6.4 fusion.41
  1570.8 10.6 reduce-scatter.35.cloned.1.call-done
  1581.4 12.7 reduce-scatter.33.cloned.1.call-done
  1594.2 8.6 fusion.42
  1602.7 12.0 add_add_fusion
  1618.2 25.2 %all-reduce = (f32[192]{0:T(256)}, f32[192]{0:T(256)}, f32[192]{0:T(256)}, f32[192]{0:T(256)}, f32[192]{0:T(256)}, /*index=5*/f32[768]{0:T(1024)}, f32[192]{0:T(256)}, f32[192]{0:T(256)}, f32[192]{0:T(256)}) all-reduce(f32[192]{0:T(256)S(1)} %convert_reduce_fusion.4, ...), channel_id=1, replica_groups=mesh['seqs'=4,'row'=2,'col'=4] {'seqs','row'}, use_global_device_ids=true, to_apply=%region_32.33 | all-reduce | flops 2304 | bytes 18432 | tf_op jit(solution)/shard_map/psum | solution.py:313
  1643.5 20.8 %all-reduce.8.cloned.1.call-done = (bf16[384,192]{0,1:T(8,128)(2,1)}, bf16[384,192]{0,1:T(8,128)(2,1)}, bf16[384,192]{0,1:T(8,128)(2,1)}, bf16[192,384]{1,0:T(8,...) async-done(((bf16[384,192]{0,1:T(8,128)(2,1)}, bf16[384,192]{0,1:T(8,128)(2,1)}, bf16[384,192]{0,1:T(8,128)(2,1)}, bf16[192,384]{1,0:T(8,128)(2,1)}, ...) | async-done | bytes 1769488 | tf_op jit(solution)/shard_map/psum | solution.py:296
  1671.5 206.9 %reduce-scatter.31.cloned.1.call-done = f32[4096,192]{0,1:T(8,128)} async-done(((f32[4096,768]{0,1:T(8,128)}), f32[4096,192]{0,1:T(8,128)}) %reduce-scatter.31.cloned.1.call-update) | async-done | bytes 3145744 | tf_op jit(solution)/shard_map/reduce_scatter | solution.py:33
  (421 shorter events, 286.9 us)
Async XLA Ops:
  7.2 121.1 %all-gather.9.cloned.1.call-start = ((), (), s32[]{:S(2)}) async-start(), calls=%async_computation.12 | async-start | bytes 7864320 | tf_op jit(solution)/shard_map/all_gather | solution.py:29
  10.1 141.8 %all-gather.11.cloned.1.call-start = ((), (), s32[]{:S(2)}) async-start(), calls=%async_computation.13 | async-start | bytes 4718592 | tf_op jit(solution)/shard_map/all_gather | solution.py:190
  133.8 25.6 %all-gather.13.cloned.1.call-start = ((), (), s32[]{:S(2)}) async-start(), calls=%async_computation.14 | async-start | bytes 4718592 | tf_op jit(solution)/shard_map/all_gather | solution.py:189
  141.9 296.8 %reduce-scatter.21.cloned.1.call-start = ((), (), s32[]{:S(2)}) async-start(), calls=%async_computation.15 | async-start | bytes 15728640 | tf_op jit(solution)/shard_map/reduce_scatter | solution.py:33
  225.5 239.2 %all-gather.17.cloned.1.call-start = ((), (), s32[]{:S(2)}) async-start(), calls=%async_computation.17 | async-start | bytes 1769472 | tf_op jit(solution)/shard_map/all_gather | solution.py:172
  227.7 233.0 %copy-start.37 = (f32[192]{0:T(256)S(1)}, f32[192]{0:T(256)}, u32[]{:S(2)}) copy-start(f32[192]{0:T(256)} %param.31) | copy-start | bytes 2308
  227.7 233.0 %copy-start.40 = (f32[192]{0:T(256)S(1)}, f32[192]{0:T(256)}, u32[]{:S(2)}) copy-start(f32[192]{0:T(256)} %param.32) | copy-start | bytes 2308
  227.7 348.6 %all-gather.15.cloned.1.call-start = ((), (), s32[]{:S(2)}) async-start(), calls=%async_computation.16 | async-start | bytes 7864320 | tf_op jit(solution)/shard_map/all_gather | solution.py:29
  441.8 823.5 %copy-start = (f32[4096,192]{0,1:T(8,128)}, f32[4096,192]{0,1:T(8,128)S(1)}, u32[]{:S(2)}) copy-start(f32[4096,192]{0,1:T(8,128)S(1)} %get-tuple-element.246) | copy-start | bytes 9437188
  460.7 804.6 %copy-start.21 = (f32[4096]{0:T(1024)}, f32[4096]{0:T(1024)S(1)}, u32[]{:S(2)}) copy-start(f32[4096]{0:T(1024)S(1)} %get-tuple-element.258) | copy-start | bytes 49156
  460.7 804.6 %copy-start.23 = (f32[4096]{0:T(1024)}, f32[4096]{0:T(1024)S(1)}, u32[]{:S(2)}) copy-start(f32[4096]{0:T(1024)S(1)} %get-tuple-element.259) | copy-start | bytes 49156
  462.5 149.4 %all-gather.19.cloned.1.call-start = ((), (), s32[]{:S(2)}) async-start(), calls=%async_computation.18 | async-start | bytes 1769472 | tf_op jit(solution)/shard_map/all_gather | solution.py:174
  464.7 367.8 %reduce-scatter.23.cloned.1.call-start = ((), (), s32[]{:S(2)}) async-start(), calls=%async_computation.19 | async-start | bytes 15728640 | tf_op jit(solution)/shard_map/reduce_scatter | solution.py:33
  622.2 375.9 %all-gather.21.cloned.1.call-start = ((), (), s32[]{:S(2)}) async-start(), calls=%async_computation.20 | async-start | bytes 7864320 | tf_op jit(solution)/shard_map/all_gather | solution.py:29
  883.0 355.8 %reduce-scatter.25.cloned.1.call-start = ((), (), s32[]{:S(2)}) async-start(), calls=%async_computation.21 | async-start | bytes 15728640 | tf_op jit(solution)/shard_map/reduce_scatter | solution.py:33
  1028.6 355.0 %all-gather.23.cloned.1.call-start = ((), (), s32[]{:S(2)}) async-start(), calls=%async_computation.22 | async-start | bytes 7864320 | tf_op jit(solution)/shard_map/all_gather | solution.py:29
  1269.8 247.5 %reduce-scatter.27.cloned.1.call-start = ((), (), s32[]{:S(2)}) async-start(), calls=%async_computation.23 | async-start | bytes 4718592 | tf_op jit(solution)/shard_map/reduce_scatter | solution.py:252
  1500.8 24.9 %reduce-scatter.29.cloned.1.call-start = ((), (), s32[]{:S(2)}) async-start(), calls=%async_computation.24 | async-start | bytes 4718592 | tf_op jit(solution)/shard_map/reduce_scatter | solution.py:255
  1502.0 59.0 %reduce-scatter.43.cloned.1.call-start = ((), (), s32[]{:S(2)}) async-start(), calls=%async_computation.31 | async-start | bytes 589824
  1509.2 53.5 %reduce-scatter.37.cloned.1.call-start = ((), (), s32[]{:S(2)}) async-start(), calls=%async_computation.28 | async-start | bytes 589824
  1517.2 47.3 %reduce-scatter.39.cloned.1.call-start = ((), (), s32[]{:S(2)}) async-start(), calls=%async_computation.29 | async-start | bytes 589824
  1525.7 43.4 %reduce-scatter.41.cloned.1.call-start = ((), (), s32[]{:S(2)}) async-start(), calls=%async_computation.30 | async-start | bytes 589824
  1534.5 46.9 %reduce-scatter.35.cloned.1.call-start = ((), (), s32[]{:S(2)}) async-start(), calls=%async_computation.27 | async-start | bytes 1769472 | tf_op jit(solution)/shard_map/reduce_scatter | solution.py:291
  1544.4 49.7 %reduce-scatter.33.cloned.1.call-start = ((), (), s32[]{:S(2)}) async-start(), calls=%async_computation.26 | async-start | bytes 1769472 | tf_op jit(solution)/shard_map/reduce_scatter | solution.py:285
  1554.4 109.8 %all-reduce.8.cloned.1.call-start = ((), (), s32[]{:S(2)}) async-start(), calls=%async_computation.32 | async-start | bytes 3538944 | tf_op jit(solution)/shard_map/psum | solution.py:296
  1594.1 284.4 %reduce-scatter.31.cloned.1.call-start = ((), (), s32[]{:S(2)}) async-start(), calls=%async_computation.25 | async-start | bytes 15728640 | tf_op jit(solution)/shard_map/reduce_scatter | solution.py:33
  1617.8 260.7 %copy-start.1 = (f32[4096,192]{0,1:T(8,128)S(1)}, f32[4096,192]{0,1:T(8,128)}, u32[]{:S(2)}) copy-start(f32[4096,192]{0,1:T(8,128)} %copy-done) | copy-start | bytes 9437188
  1617.8 260.7 %copy-start.22 = (f32[4096]{0:T(1024)S(1)}, f32[4096]{0:T(1024)}, u32[]{:S(2)}) copy-start(f32[4096]{0:T(1024)} %copy-done.21) | copy-start | bytes 49156
  1617.8 260.7 %copy-start.24 = (f32[4096]{0:T(1024)S(1)}, f32[4096]{0:T(1024)}, u32[]{:S(2)}) copy-start(f32[4096]{0:T(1024)} %copy-done.23) | copy-start | bytes 49156
  1617.8 260.7 %copy-start.30 = (f32[4096]{0:T(1024)S(1)}, f32[4096]{0:T(1024)}, u32[]{:S(2)}) copy-start(f32[4096]{0:T(1024)} %copy-done.29) | copy-start | bytes 49156
  1617.8 260.7 %copy-start.36 = (f32[4096]{0:T(1024)S(1)}, f32[4096]{0:T(1024)}, u32[]{:S(2)}) copy-start(f32[4096]{0:T(1024)} %copy-done.35) | copy-start | bytes 49156
  1617.9 260.7 %copy-start.38 = (f32[192]{0:T(256)S(1)}, f32[192]{0:T(256)}, u32[]{:S(2)}) copy-start(f32[192]{0:T(256)} %param.31) | copy-start | bytes 2308
  (44 other events, 1334.2 us)
Sparse Core Ops, SparseCore 0:
  10.2 118.0 all-gather.8
  133.9 10.5 all-gather.10
  146.0 13.3 all-gather.12
  225.6 213.0 reduce-scatter.20
  440.7 10.2 all-gather.16
  462.6 113.6 all-gather.14
  578.4 7.3 all-gather.18
  622.4 210.0 reduce-scatter.22
  883.1 114.9 all-gather.20
  1028.8 210.0 reduce-scatter.24
  1269.9 113.6 all-gather.22
  1501.0 9.1 reduce-scatter.26
  1512.4 12.2 reduce-scatter.28
  1526.7 9.0 reduce-scatter.42
  1538.0 8.9 reduce-scatter.36
  1549.0 8.9 reduce-scatter.38
  1560.1 8.9 reduce-scatter.40
  1571.7 9.6 reduce-scatter.34
  1584.2 9.7 reduce-scatter.32
  1598.3 65.8 all-reduce.7
  1666.6 211.8 reduce-scatter.30
where the time goes:
time: 1900 us; the launch traced here: 1890 us
  waiting for transfers between devices  1340 us (71%)
  matrix products  239 us (13%)
  blocking collectives  106 us (6%)
  other arithmetic  92.2 us (5%)
  local copies, waits for them, and re-layouts  91 us (5%)
    reduce_scatter x4, waiting for transfers between devices, reduce_cols(): lax.psum_scatter(partial_term, 'col', scatter_dimension=1, tiled=True)  833 us
    all_gather x4, waiting for transfers between devices, spread_cols(): return lax.all_gather(local_piece, 'col', axis=1, tiled=True)  456 us
    psum x4, blocking collectives, pair_sums(): return lax.psum((sum_one, sum_two), 'col')  72.7 us
    dot_general x6, matrix products, against(): lax.dot_general(left_side, right_side, (((1,), (1,)), ((), ())), preferre...  52.2 us
    dynamic_slice x64, local copies, waits for them, and re-layouts, local(): lax.map(attend_block, (blocks_of(query_seq, group_size), blocks_of(key_ro...  43.1 us
    dot_general x6, matrix products, inner(): lax.dot_general(left_side, right_side, (((0,), (0,)), ((), ())), preferre...  41.1 us
  transfers between devices with their start and end apart: 21, of which 13 were waited for; matrix products, arithmetic and copies ran while one was open for 8% of the time, Pallas kernels for 0%

commit v1 on v0

v1 whole, which is shorter than its diff:
```python
from functools import partial
import math

import jax
import jax.numpy as jnp
from jax import lax
from jax.experimental import pallas as pl
from jax.experimental.pallas import tpu as pltpu
from jax.sharding import PartitionSpec as P

HD = 64
EXTRA = 16

epsilon = 1e-05
masked = -1e30
low = jnp.bfloat16
SCALE = 1.0 / math.sqrt(HD)


def dot_nn(a, b):
    return lax.dot_general(a, b, (((1,), (0,)), ((), ())), preferred_element_type=jnp.float32)


def dot_tn(a, b):
    return lax.dot_general(a, b, (((0,), (0,)), ((), ())), preferred_element_type=jnp.float32)


def dot_nt(a, b):
    return lax.dot_general(a, b, (((1,), (1,)), ((), ())), preferred_element_type=jnp.float32)


def extra_rows(width, rows):
    index = lax.broadcasted_iota(jnp.int32, (EXTRA, width), 0)
    total = jnp.zeros((EXTRA, width), jnp.float32)
    for at, row in enumerate(rows):
        total = jnp.where(index == at, row, total)
    return total.astype(low)


def three_terms(row):
    high = row.astype(low).astype(jnp.float32)
    rest = row - high
    mid = rest.astype(low).astype(jnp.float32)
    return [high, mid, rest - mid]


def key_bias(keys, limit):
    position = lax.broadcasted_iota(jnp.int32, (1, keys), 1)
    return jnp.where(position < limit, 0.0, masked)


def attend_kernel(step, lens, q_ref, k_ref, v_ref, o_ref, lse_ref):
    queries, keys = q_ref.shape[1], k_ref.shape[1]
    one = jnp.ones((1, 1), jnp.float32)
    bias = key_bias(keys, lens[pl.program_id(0)])
    key_side = jnp.concatenate([k_ref[...], extra_rows(keys, [bias])], axis=0)
    value_side = jnp.concatenate([v_ref[...], extra_rows(keys, [one])], axis=0)
    for start in range(0, queries, step):
        part = pl.ds(start, step)
        query_side = jnp.concatenate([q_ref[:, part] * SCALE, extra_rows(step, [one])], axis=0)
        scores = dot_tn(key_side, query_side)
        peak = jnp.max(scores, axis=0, keepdims=True)
        probs = jnp.exp(scores - peak).astype(low)
        mixed = dot_nn(value_side, probs)
        total = mixed[HD : HD + 1]
        o_ref[:, part] = (mixed[:HD] / total).astype(low)
        lse_ref[0, :, part] = peak + jnp.log(total)


def attend_back_kernel(step, lens, q_ref, k_ref, v_ref, o_ref, lse_ref, g_ref, dq_ref, dk_ref, dv_ref, dk_sum, dv_sum):
    queries, keys = q_ref.shape[1], k_ref.shape[1]
    one = jnp.ones((1, 1), jnp.float32)
    bias = key_bias(keys, lens[pl.program_id(0)])
    key_side = jnp.concatenate([k_ref[...], extra_rows(keys, [bias, one, one, one])], axis=0)
    value_side = jnp.concatenate([v_ref[...], extra_rows(keys, [one, one, one])], axis=0)
    for start in range(0, queries, step):
        part = pl.ds(start, step)
        query, grad = q_ref[:, part] * SCALE, g_ref[:, part]
        delta = jnp.sum(
            grad.astype(jnp.float32) * o_ref[:, part].astype(jnp.float32), axis=0, keepdims=True
        )
        query_side = jnp.concatenate(
            [query, extra_rows(step, [one] + three_terms(-lse_ref[0, :, part]))], axis=0
        )
        grad_side = jnp.concatenate([grad, extra_rows(step, three_terms(-delta))], axis=0)
        probs = jnp.exp(dot_tn(key_side, query_side))
        grad_scores = (probs * dot_tn(value_side, grad_side)).astype(low)
        dq_ref[:, part] = (dot_nn(k_ref[...], grad_scores) * SCALE).astype(low)
        dk_part = dot_nt(query, grad_scores)
        dv_part = dot_nt(grad, probs.astype(low))
        if start == 0:
            dk_sum[...] = dk_part
            dv_sum[...] = dv_part
        else:
            dk_sum[...] += dk_part
            dv_sum[...] += dv_part
    dk_ref[...] = dk_sum[...].astype(low)
    dv_ref[...] = dv_sum[...].astype(low)


def query_step(queries, keys):
    for step in (256, 128):
        if queries % step == 0 and step * keys <= 2**20:
            return step
    return queries


def attention(lengths, q, k, v, count):
    rows, tokens = q.shape
    queries, keys = tokens // count, k.shape[1] // count
    heads = rows // HD
    step = query_step(queries, keys)
    spec = lambda size: pl.BlockSpec((HD, size), lambda b, h, lens: (h, b))
    return pl.pallas_call(
        partial(attend_kernel, step),
        grid_spec=pltpu.PrefetchScalarGridSpec(
            num_scalar_prefetch=1,
            grid=(count, heads),
            in_specs=[spec(queries), spec(keys), spec(keys)],
            out_specs=[spec(queries), pl.BlockSpec((1, 1, queries), lambda b, h, lens: (h, 0, b))],
        ),
        out_shape=(
            jax.ShapeDtypeStruct((rows, tokens), low),
            jax.ShapeDtypeStruct((heads, 1, tokens), jnp.float32),
        ),
        cost_estimate=pl.CostEstimate(
            flops=16 * rows * tokens * keys,
            bytes_accessed=8 * rows * tokens,
            transcendentals=heads * tokens * keys,
        ),
        name="attend",
    )(lengths, q, k, v)


def attention_back(lengths, q, k, v, o, lse, grad, count):
    rows, tokens = q.shape
    queries, keys = tokens // count, k.shape[1] // count
    heads = rows // HD
    step = query_step(queries, keys)
    spec = lambda size: pl.BlockSpec((HD, size), lambda b, h, lens: (h, b))
    return pl.pallas_call(
        partial(attend_back_kernel, step),
        grid_spec=pltpu.PrefetchScalarGridSpec(
            num_scalar_prefetch=1,
            grid=(count, heads),
            in_specs=[
                spec(queries),
                spec(keys),
                spec(keys),
                spec(queries),
                pl.BlockSpec((1, 1, queries), lambda b, h, lens: (h, 0, b)),
                spec(queries),
            ],
            out_specs=[spec(queries), spec(keys), spec(keys)],
            scratch_shapes=[pltpu.VMEM((HD, keys), jnp.float32)] * 2,
        ),
        out_shape=(
            jax.ShapeDtypeStruct((rows, tokens), low),
            jax.ShapeDtypeStruct(k.shape, low),
            jax.ShapeDtypeStruct(k.shape, low),
        ),
        cost_estimate=pl.CostEstimate(
            flops=40 * rows * tokens * keys,
            bytes_accessed=16 * rows * tokens,
            transcendentals=heads * tokens * keys,
        ),
        name="attend_back",
    )(lengths, q, k, v, o, lse, grad)


def up_form(weight, rows):
    product = jnp.einsum("cij,it->cjt", weight, rows, preferred_element_type=jnp.float32)
    return product.reshape(-1, rows.shape[1])


def down_form(weight, rows):
    rows = rows.reshape(weight.shape[0], weight.shape[2], rows.shape[1])
    return jnp.einsum("cij,cjt->it", weight, rows, preferred_element_type=jnp.float32)


def normalize(hidden, gain, shift):
    centre = jnp.mean(hidden, axis=0, keepdims=True)
    inverse = lax.rsqrt(jnp.mean(hidden * hidden, axis=0, keepdims=True) - centre * centre + epsilon)
    normed = (hidden - centre) * inverse
    return normed * gain + shift, normed, inverse


def norm_back(grad_out, normed, inverse, gain):
    scaled = grad_out * gain
    return inverse * (
        scaled
        - jnp.mean(scaled, axis=0, keepdims=True)
        - normed * jnp.mean(scaled * normed, axis=0, keepdims=True)
    )


def spread(piece):
    seqs, row, col = (lax.axis_size(name) for name in ("seqs", "row", "col"))
    height = piece.shape[0]
    if height % (16 * seqs) == 0:
        share = height // seqs
        piece = lax.dynamic_slice_in_dim(piece, lax.axis_index("seqs") * share, share, 0)
        whole = lax.all_gather(piece, ("col", "row", "seqs"), axis=0, tiled=True)
    else:
        whole = lax.all_gather(piece, ("col", "row"), axis=0, tiled=True)
    return whole.reshape(col, row * height, piece.shape[1])


def collect(grad):
    seqs = lax.axis_size("seqs")
    grad = lax.psum_scatter(grad.astype(low), "row", scatter_dimension=0, tiled=True)
    if grad.shape[0] % (16 * seqs) == 0:
        grad = lax.psum_scatter(grad, "seqs", scatter_dimension=0, tiled=True)
        grad = lax.psum_scatter(grad, "col", scatter_dimension=1, tiled=True)
        return lax.all_gather(grad, "seqs", axis=0, tiled=True)
    grad = lax.psum_scatter(grad, "col", scatter_dimension=1, tiled=True)
    return lax.psum(grad, "seqs")


def local(
    tokens,
    lengths,
    query_weight,
    query_bias,
    key_weight,
    value_weight,
    value_bias,
    out_weight,
    out_bias,
    first_gain,
    first_shift,
    up_weight,
    up_bias,
    down_weight,
    down_bias,
    second_gain,
    second_shift,
    cotangent,
):
    seq_count, width, rows = tokens.shape
    row, col = lax.axis_size("row"), lax.axis_size("col")
    row_at, col_at = lax.axis_index("row"), lax.axis_index("col")
    members = row * col
    full = width * col
    alone = seq_count % members == 0
    if alone:
        count = seq_count // members
        mine = row * rows
        first = jnp.int32(0)
        own_lengths = lax.dynamic_slice_in_dim(lengths, (col_at * row + row_at) * count, count, 0)
    else:
        count = seq_count // col
        mine = rows
        first = row_at * rows
        own_lengths = lax.dynamic_slice_in_dim(lengths, col_at * count, count, 0)

    def enter(array):
        if alone:
            array = lax.all_to_all(array, ("col", "row"), split_axis=0, concat_axis=0, tiled=True)
            array = array.reshape(col, row, count, width, rows)
            return jnp.transpose(array, (0, 3, 2, 1, 4)).reshape(full, count * mine)
        array = lax.all_to_all(array, "col", split_axis=0, concat_axis=0, tiled=True)
        array = array.reshape(col, count, width, rows)
        return jnp.transpose(array, (0, 2, 1, 3)).reshape(full, count * mine)

    def leave(array):
        if alone:
            array = array.reshape(col, width, count, row, rows)
            array = jnp.transpose(array, (0, 3, 2, 1, 4)).reshape(seq_count, width, rows)
            return lax.all_to_all(array, ("col", "row"), split_axis=0, concat_axis=0, tiled=True)
        array = jnp.transpose(array.reshape(col, width, count, mine), (0, 2, 1, 3))
        array = array.reshape(seq_count, width, rows)
        return lax.all_to_all(array, "col", split_axis=0, concat_axis=0, tiled=True)

    def by_sequence(move, array):
        parts = [move(part) for part in jnp.split(array, count, axis=1)]
        return jnp.concatenate(parts, axis=1)

    def all_keys(array):
        if alone:
            return array
        return by_sequence(lambda part: lax.all_gather(part, "row", axis=1, tiled=True), array)

    def own_keys(array):
        if alone:
            return array
        return by_sequence(
            lambda part: lax.psum_scatter(part, "row", scatter_dimension=1, tiled=True), array
        )

    x_low = enter(tokens)
    qkv_piece = jnp.concatenate([query_weight, key_weight, value_weight], axis=1).astype(low)
    qkv_full = spread(qkv_piece)
    out_full = spread(out_weight.T.astype(low))
    up_full = spread(up_weight.astype(low))
    down_full = spread(down_weight.astype(low))
    small = jnp.concatenate(
        [
            query_bias,
            value_bias,
            out_bias,
            first_gain,
            first_shift,
            down_bias,
            second_gain,
            second_shift,
            up_bias,
        ]
    )
    small = lax.all_gather(small, "col", axis=0, tiled=False)
    vectors = [small[:, at * width : (at + 1) * width].reshape(full, 1) for at in range(8)]
    qb, vb, ob, gain1, shift1, db, gain2, shift2 = vectors
    ub = small[:, 8 * width :].reshape(-1, 1)

    token_count = count * mine
    qkv = up_form(qkv_full, x_low).reshape(col, 3, width, token_count)
    q = (qkv[:, 0].reshape(full, token_count) + qb).astype(low)
    k = qkv[:, 1].reshape(full, token_count).astype(low)
    v = (qkv[:, 2].reshape(full, token_count) + vb).astype(low)
    k_all, v_all = all_keys(k), all_keys(v)
    mixed, lse = attention(own_lengths, q, k_all, v_all, count)
    h1 = x_low.astype(jnp.float32) + (down_form(out_full, mixed) + ob)
    y1, n1, inv1 = normalize(h1, gain1, shift1)
    y1_low = y1.astype(low)
    pre = up_form(up_full, y1_low) + ub
    act, gelu_back = jax.vjp(partial(jax.nn.gelu, approximate=False), pre)
    act_low = act.astype(low)
    h2 = y1 + (down_form(down_full, act_low) + db)
    out, n2, inv2 = normalize(h2, gain2, shift2)
    layer_output = leave(out.astype(low))

    position = first + jnp.arange(mine, dtype=jnp.int32)
    valid = (position[None, :] < own_lengths[:, None]).astype(jnp.float32).reshape(1, token_count)
    g = enter(cotangent).astype(jnp.float32) * valid
    gain2_grad = jnp.sum(g * n2, axis=1)
    shift2_grad = jnp.sum(g, axis=1)
    dh2 = norm_back(g, n2, inv2, gain2)
    dz = dh2.astype(low)
    db_grad = jnp.sum(dz, axis=1, dtype=jnp.float32)
    down_grad = collect(dot_nt(dz, act_low))
    dpre = gelu_back(up_form(down_full, dz))[0].astype(low)
    ub_grad = jnp.sum(dpre, axis=1, dtype=jnp.float32)
    up_grad = collect(dot_nt(y1_low, dpre))
    dy1 = dh2 + down_form(up_full, dpre)
    gain1_grad = jnp.sum(dy1 * n1, axis=1)
    shift1_grad = jnp.sum(dy1, axis=1)
    dh1 = norm_back(dy1, n1, inv1, gain1)
    da = dh1.astype(low)
    ob_grad = jnp.sum(da, axis=1, dtype=jnp.float32)
    out_grad = collect(dot_nt(da, mixed))
    grad_mixed = up_form(out_full, da).astype(low)
    dq, dk, dv = attention_back(own_lengths, q, k_all, v_all, mixed, lse, grad_mixed, count)
    dk, dv = own_keys(dk), own_keys(dv)
    qb_grad = jnp.sum(dq, axis=1, dtype=jnp.float32)
    vb_grad = jnp.sum(dv, axis=1, dtype=jnp.float32)
    block = lambda array: array.reshape(col, width, token_count)
    dqkv = jnp.stack([block(dq), block(dk), block(dv)], axis=1).reshape(3 * full, token_count)
    dx = dh1 + down_form(qkv_full, dqkv)
    tokens_grad = leave(dx.astype(low))
    qkv_grad = collect(dot_nt(x_low, dqkv)).astype(jnp.float32)
    vectors = [qb_grad, vb_grad, ob_grad, gain1_grad, shift1_grad, db_grad, gain2_grad, shift2_grad]
    vectors = [vector.reshape(col, width) for vector in vectors] + [ub_grad.reshape(col, -1)]
    small_grad = lax.psum(jnp.concatenate(vectors, axis=1), ("seqs", "row", "col"))
    small_grad = lax.dynamic_index_in_dim(small_grad, col_at, 0, keepdims=False)
    pieces = [small_grad[at * width : (at + 1) * width] for at in range(8)]
    return (
        layer_output,
        tokens_grad,
        qkv_grad[:, :width],
        pieces[0],
        qkv_grad[:, width : 2 * width],
        qkv_grad[:, 2 * width :],
        pieces[1],
        out_grad.astype(jnp.float32).T,
        pieces[2],
        pieces[3],
        pieces[4],
        up_grad.astype(jnp.float32),
        small_grad[8 * width :],
        down_grad.astype(jnp.float32),
        pieces[5],
        pieces[6],
        pieces[7],
    )


def solution(mesh):
    wide, vector = P("seqs", "col", "row"), P("col")
    square, turned = P("row", "col"), P("col", "row")
    in_specs = (
        wide,
        P("seqs"),
        square,
        vector,
        square,
        square,
        vector,
        turned,
        vector,
        vector,
        vector,
        square,
        vector,
        square,
        vector,
        vector,
        vector,
        wide,
    )
    out_specs = (
        wide,
        wide,
        square,
        vector,
        square,
        square,
        vector,
        turned,
        vector,
        vector,
        vector,
        square,
        vector,
        square,
        vector,
        vector,
        vector,
    )
    return jax.shard_map(local, mesh=mesh, in_specs=in_specs, out_specs=out_specs, check_vma=False)
```

time: 1900 us -> 706 us (0.37)
  waiting for transfers between devices: 1340 us -> 182 us
  matrix products: 239 us -> 127 us
  Pallas kernels: 0 us -> 78.1 us
  other arithmetic: 92.2 us -> 21.1 us
  blocking collectives: 106 us -> 174 us
    reduce_scatter x8 -> x9, waiting for transfers between devices: 856 us -> 119 us  [the longest x3 90.3 us: collect(): grad = lax.psum_scatter(grad, 'seqs', scatter_dimension=0, tiled=True)]
    all_gather x8 -> x4, waiting for transfers between devices: 464 us -> 37.9 us  [spread(): whole = lax.all_gather(piece, ('col', 'row', 'seqs'), axis=0, tiled=True)]
    dot_general x74 -> x12, matrix products: 239 us -> 127 us  [the longest x4 66.4 us: up_form(): jnp.einsum('cij,it->cjt', weight, rows, preferred_element_type=jnp.float32)]
    pallas_call x0 -> x2, Pallas kernels: none -> 78.1 us  [the longest x1 40.6 us: attention_back(): pl.pallas_call(partial(attend_back_kernel, step), grid_spec=pltpu.Prefetc...]
    all_gather x4 -> x5, blocking collectives: 8.4 us -> 86.3 us  [the longest x1 44 us: local(): small = lax.all_gather(small, 'col', axis=0, tiled=False)]
    psum x5 -> x1, blocking collectives: 97.9 us -> 39.7 us  [local(): lax.psum(jnp.concatenate(vectors, axis=1), ('seqs', 'row', 'col'))]
    all_to_all x0 -> x1, blocking collectives: none -> 48.4 us  [enter(): lax.all_to_all(array, ('col', 'row'), split_axis=0, concat_axis=0, tiled=...]
    dynamic_slice x64 -> x4, local copies, waits for them, and re-layouts: 43.1 us -> 3.26 us  [the longest x3 2.68 us: spread(): lax.dynamic_slice_in_dim(piece, lax.axis_index('seqs') * share, share, 0)]
  transfers between devices with their start and end apart: 21 -> 19, of which waited for: 13 -> 12; matrix products, arithmetic and copies ran while one was open for 8% -> 23% of each run, Pallas kernels for 0% -> 11%
where the time goes in v1:
time: 706 us; the launch traced here: 698 us
  waiting for transfers between devices  182 us (26%)
  blocking collectives  174 us (25%)
  matrix products  127 us (18%)
  local copies, waits for them, and re-layouts  86.3 us (12%)
  Pallas kernels  78.1 us (11%)
  other arithmetic  21.1 us (3%)
  between operations  15.1 us (2%)
  starting transfers between devices  13.6 us (2%)
    reduce_scatter x3, waiting for transfers between devices, collect(): grad = lax.psum_scatter(grad, 'seqs', scatter_dimension=0, tiled=True)  90.3 us
    dot_general x4, matrix products, up_form(): jnp.einsum('cij,it->cjt', weight, rows, preferred_element_type=jnp.float32)  66.4 us
    all_to_all x1, blocking collectives, enter(): lax.all_to_all(array, ('col', 'row'), split_axis=0, concat_axis=0, tiled=...  48.4 us
    all_gather x1, blocking collectives, local(): small = lax.all_gather(small, 'col', axis=0, tiled=False)  44 us
    all_gather x4, blocking collectives, collect(): return lax.all_gather(grad, 'seqs', axis=0, tiled=True)  42.3 us
    pallas_call x1, Pallas kernels, attention_back(): pl.pallas_call(partial(attend_back_kernel, step), grid_spec=pltpu.Prefetc...  40.6 us
    psum x1, blocking collectives, local(): lax.psum(jnp.concatenate(vectors, axis=1), ('seqs', 'row', 'col'))  39.7 us
    all_gather x4, waiting for transfers between devices, spread(): whole = lax.all_gather(piece, ('col', 'row', 'seqs'), axis=0, tiled=True)  37.9 us
  transfers between devices with their start and end apart: 19, of which 12 were waited for; matrix products, arithmetic and copies ran while one was open for 23% of the time, Pallas kernels for 11%

profile of v1, /device:TPU:0, one launch (start us, length us, event | category | flops | bytes accessed | tf_op | source)
XLA Modules:
  0.0 697.8 jit_solution(16227842160490684142)
XLA Ops:
  14.3 48.4 %all_to_all.20 = bf16[8,192,512]{2,1,0:T(8,128)(2,1)} all-to-all(bf16[8,192,512]{2,1,0:T(8,128)(2,1)S(1)} %copy-done.16), channel_id=1, replica_groups=mesh['seqs'=4,'row'=2,'col'=4] {'col','row'}, dimensions={0} | all-to-all | bytes 3145728 | tf_op jit(solution)/shard_map/all_to_all | solution.py:259
  68.2 44.0 %all-gather.1 = f32[4,1,2304]{2,1,0:T(1,128)S(1)} all-gather(f32[1,1,2304]{2,1,0:T(1,128)S(1)} %reshape.260), channel_id=2, replica_groups=mesh['seqs'=4,'row'=2,'col'=4] {'col'}, dimensions={0}, use_global_device_ids=true | all-gather | bytes 46080 | tf_op jit(solution)/shard_map/all_gather | solution.py:310
  133.6 14.0 %all-gather.9.cloned.1.call-done = bf16[3072,576]{1,0:T(8,128)(2,1)} async-done(((bf16[96,576]{1,0:T(8,128)(2,1)}), bf16[3072,576]{1,0:T(8,128)(2,1)}) %all-gather.9.cloned.1.call-update) | async-done | bytes 3538960 | tf_op jit(solution)/shard_map/all_gather | solution.py:203
  147.6 8.2 %copy.117 = bf16[4,768,576]{1,0,2:T(4,128)(2,1)} copy(bf16[4,768,576]{2,1,0:T(8,128)(2,1)} %bitcast.145) | data formatting | bytes 7077888 | tf_op jit(solution)/shard_map/reshape | solution.py:206
  167.0 37.6 %attend.1 = (bf16[768,1024]{1,0:T(8,128)(2,1)}, f32[12,1,1024]{2,1,0:T(1,128)}) custom-call(s32[1]{0:T(128)} %dynamic_slice.20.lens, bf16[768,1024]{1,0:T(8,128)(2,1)} %get-tuple-element.165.q_ref, bf16[768,1024]{1,0:T(8,128)(2,1)} %bitcast.151, bf16[768,1024]{1,0:T(8,128)(2,1)} %get-tuple-element.164.v_ref), custom_call_target="tpu_custom_call" | custom-call | flops 12884901888 | bytes 6291456 | tf_op jit(solution)/shard_map/attend/pallas_call | solution.py:114
  204.6 5.8 fusion.28
  213.5 6.6 copy.99
  220.1 37.8 %multiply_convert_fusion = (bf16[3072,1024]{1,0:T(8,128)(2,1)}, f32[3072,1024]{1,0:T(8,128)}, f32[3072,1024]{1,0:T(8,128)}) fusion(f32[3072]{0:T(1024)S(1)} %add.158, bf16[3072,768]{1,0:T(8,128)(2,1)} %bitcast.143, f32[768,1024]{1,0:T(8,128)} %get-tuple-element.158, f32[768]{0:T(1024)S(1)} %add.155, f32[768]{0:T(1024)S(1)} %mul.177, ...), kind=kOutput, calls=%fused_computation.4 | convolution fusion | flops 5043388416 | bytes 39348224 | tf_op jit(solution)/shard_map/cij,it->cjt/dot_general | solution.py:172
  258.0 20.8 %all-gather.11.cloned.1.call-done = bf16[3072,768]{1,0:T(8,128)(2,1)} async-done(((bf16[96,768]{1,0:T(8,128)(2,1)}), bf16[3072,768]{1,0:T(8,128)(2,1)}) %all-gather.11.cloned.1.call-update) | async-done | bytes 4718608 | tf_op jit(solution)/shard_map/all_gather | solution.py:203
  278.8 9.6 %fusion.27 = (f32[1024]{0:T(1024)S(1)}, f32[1024]{0:T(1024)S(1)}, f32[768,1024]{1,0:T(8,128)S(1)}) fusion(f32[768]{0:T(1024)S(1)} %add.161, bf16[4,768,768]{2,1,0:T(8,128)(2,1)} %bitcast.138, bf16[4,768,1024]{2,1,0:T(8,128)(2,1)} %bitcast.169, f32[768]{0:T(1024)S(1)} %add.155, f32[768]{0:T(1024)S(1)} %mul.177, f32[1024]{0:T(1024)S(1)} %get-tuple-element.157, ...), kind=kOutput, calls=%fused_computation.91 | convolution fusion | flops 4838914048 | bytes 17327104 | tf_op jit(solution)/shard_map/cij,cjt->it/dot_general | solution.py:178
  291.2 6.6 copy.102
  297.9 4.4 convert_reduce_fusion.1
  302.3 20.8 %convert_reduce_fusion = (f32[3072]{0:T(1024)}, bf16[3072,1024]{1,0:T(8,128)(2,1)}) fusion(f32[3072,1024]{1,0:T(8,128)} %get-tuple-element.129, bf16[3072,768]{1,0:T(8,128)(2,1)} %bitcast.142, f32[768,1024]{1,0:T(8,128)} %get-tuple-element.125, f32[3072,1024]{1,0:T(8,128)} %get-tuple-element.159, f32[3072]{0:T(1024)S(1)} %add.158), kind=kOutput, calls=%fused_computation.2 | convolution fusion | flops 4886098944 | bytes 39346176 | tf_op jit(solution)/shard_map/cij,it->cjt/dot_general | solution.py:172
  323.1 10.4 %multiply_reduce_fusion.1 = (f32[768]{0:T(1024)}, f32[1024]{0:T(1024)S(1)}, f32[1024]{0:T(1024)S(1)}, f32[768]{0:T(1024)}, f32[768,1024]{1,0:T(8,128)S(1)}) fusion(f32[768,1024]{1,0:T(8,128)S(1)} %copy-done.10, f32[1024]{0:T(1024)S(1)} %get-tuple-element.157, f32[1024]{0:T(1024)S(1)} %get-tuple-element.156, f32[768]{0:T(1024)S(1)} %mul.177, ...), kind=kOutput, calls=%fused_computation.40 | convolution fusion | flops 4839698432 | bytes 20472832 | tf_op jit(solution)/shard_map/cij,cjt->it/dot_general | solution.py:178
  341.2 40.6 %attend_back.1 = (bf16[768,1024]{1,0:T(8,128)(2,1)}, bf16[768,1024]{1,0:T(8,128)(2,1)}, bf16[768,1024]{1,0:T(8,128)(2,1)}) custom-call(s32[1]{0:T(128)} %dynamic_slice.20.lens, bf16[768,1024]{1,0:T(8,128)(2,1)} %get-tuple-element.165.q_ref, bf16[768,1024]{1,0:T(8,128)(2,1)} %bitcast.152, bf16[768,1024]{1,0:T(8,128)(2,1)} %get-tuple-element.164.v_ref, ...), custom_call_target="tpu_custom_call" | custom-call | flops 32212254720 | bytes 12582912 | tf_op jit(solution)/shard_map/attend_back/pallas_call | solution.py:141
  386.7 4.1 fusion.6
  396.7 9.7 %convolution_convert_fusion = bf16[768,3072]{1,0:T(8,128)(2,1)} fusion(bf16[3072,1024]{1,0:T(8,128)(2,1)} %get-tuple-element.128, f32[768,1024]{1,0:T(8,128)S(1)} %copy-done.15), kind=kOutput, calls=%fused_computation.18 | convolution fusion | flops 4834983936 | bytes 14155776 | tf_op jit(solution)/shard_map/dot_general | solution.py:29
  408.3 10.1 %convolution_convert_fusion.1 = bf16[768,3072]{1,0:T(8,128)(2,1)} fusion(bf16[3072,1024]{1,0:T(8,128)(2,1)} %get-tuple-element.163, f32[768,1024]{1,0:T(8,128)S(1)} %copy-done.11, f32[768]{0:T(1024)S(1)} %copy-done.32, f32[768]{0:T(1024)S(1)} %mul.177, f32[1024]{0:T(1024)S(1)} %copy-done.27, f32[1024]{0:T(1024)S(1)} %copy-done.25), kind=kOutput, calls=%fused_computation.19 | convolution fusion | flops 4838129664 | bytes 14170112 | tf_op jit(solution)/shard_map/dot_general | solution.py:29
  421.4 16.1 %reduce-scatter.25.cloned.1.call-done = bf16[384,3072]{1,0:T(8,128)(2,1)} async-done(((bf16[768,3072]{1,0:T(8,128)(2,1)}), bf16[384,3072]{1,0:T(8,128)(2,1)}) %reduce-scatter.25.cloned.1.call-update) | async-done | bytes 2359312 | tf_op jit(solution)/shard_map/reduce_scatter | solution.py:211
  437.6 8.5 %fusion.7 = bf16[768,1024]{1,0:T(8,128)(2,1)} fusion(f32[768,1024]{1,0:T(8,128)S(1)} %copy-done.13, bf16[4,768,576]{2,1,0:T(8,128)(2,1)} %bitcast.146, bf16[4,576,1024]{2,1,0:T(8,128)(2,1)} %bitcast.141), kind=kOutput, calls=%fused_computation.25 | convolution fusion | flops 3625451520 | bytes 12976128 | tf_op jit(solution)/shard_map/cij,cjt->it/dot_general | solution.py:178
  450.4 5.0 all-to-all-start.3
  455.4 11.7 %reduce-scatter.23.cloned.1.call-done = bf16[96,768]{1,0:T(8,128)(2,1)} async-done(((bf16[384,768]{1,0:T(8,128)(2,1)}), bf16[96,768]{1,0:T(8,128)(2,1)}) %reduce-scatter.23.cloned.1.call-update) | async-done | bytes 147472 | tf_op jit(solution)/shard_map/reduce_scatter | solution.py:213
  473.2 20.0 %all-to-all-done.3 = bf16[8,192,512]{2,1,0:T(8,128)(2,1)S(1)} async-done(((bf16[8,192,512]{2,1,0:T(8,128)(2,1)}), bf16[8,192,512]{2,1,0:T(8,128)(2,1)S(1)}, u32[]{:S(2)}, u32[]{:S(2)}) %all-to-all-start.3) | async-done | bytes 1572896 | tf_op jit(solution)/shard_map/all_to_all | solution.py:270
  494.3 4.4 all-to-all-start.1
  504.7 38.3 %reduce-scatter.33.cloned.1.call-done = bf16[96,3072]{1,0:T(8,128)(2,1)} async-done(((bf16[384,3072]{1,0:T(8,128)(2,1)}), bf16[96,3072]{1,0:T(8,128)(2,1)}) %reduce-scatter.33.cloned.1.call-update) | async-done | bytes 589840 | tf_op jit(solution)/shard_map/reduce_scatter | solution.py:213
  543.1 40.2 %reduce-scatter.27.cloned.1.call-done = bf16[96,3072]{1,0:T(8,128)(2,1)} async-done(((bf16[384,3072]{1,0:T(8,128)(2,1)}), bf16[96,3072]{1,0:T(8,128)(2,1)}) %reduce-scatter.27.cloned.1.call-update) | async-done | bytes 589840 | tf_op jit(solution)/shard_map/reduce_scatter | solution.py:213
  584.6 39.7 %psum.7 = f32[4,2304]{1,0:T(4,128)S(1)} all-reduce(f32[4,2304]{1,0:T(4,128)S(1)} %concatenate.12), channel_id=1, replica_groups=mesh['seqs'=4,'row'=2,'col'=4] {'seqs','row','col'}, use_global_device_ids=true, to_apply=%region_20.0 | all-reduce | flops 9216 | bytes 73728 | tf_op jit(solution)/shard_map/psum | solution.py:363
  626.6 9.6 %all_gather.37 = bf16[384,192]{1,0:T(8,128)(2,1)S(1)} all-gather(bf16[96,192]{1,0:T(8,128)(2,1)S(1)} %copy.124), channel_id=1, replica_groups=mesh['seqs'=4,'row'=2,'col'=4] {'seqs'}, dimensions={0}, use_global_device_ids=true | all-gather | bytes 184320 | tf_op jit(solution)/shard_map/all_gather | solution.py:215
  638.1 9.9 %all_gather.36 = bf16[384,576]{1,0:T(8,128)(2,1)S(1)} all-gather(bf16[96,576]{1,0:T(8,128)(2,1)S(1)} %copy.109), channel_id=1, replica_groups=mesh['seqs'=4,'row'=2,'col'=4] {'seqs'}, dimensions={0}, use_global_device_ids=true | all-gather | bytes 552960 | tf_op jit(solution)/shard_map/all_gather | solution.py:215
  651.7 11.4 %all_gather.39 = bf16[384,768]{1,0:T(8,128)(2,1)S(1)} all-gather(bf16[96,768]{1,0:T(8,128)(2,1)} %reduce-scatter.35.cloned.1.call-done), channel_id=1, replica_groups=mesh['seqs'=4,'row'=2,'col'=4] {'seqs'}, dimensions={0}, use_global_device_ids=true | all-gather | bytes 737280 | tf_op jit(solution)/shard_map/all_gather | solution.py:215
  664.2 10.2 %reduce-scatter.29.cloned.1.call-done = bf16[96,768]{1,0:T(8,128)(2,1)} async-done(((bf16[96,3072]{1,0:T(8,128)(2,1)}), bf16[96,768]{1,0:T(8,128)(2,1)}) %reduce-scatter.29.cloned.1.call-update) | async-done | bytes 147472 | tf_op jit(solution)/shard_map/reduce_scatter | solution.py:214
  674.4 11.5 %all_gather.38 = bf16[384,768]{1,0:T(8,128)(2,1)S(1)} all-gather(bf16[96,768]{1,0:T(8,128)(2,1)} %reduce-scatter.29.cloned.1.call-done), channel_id=1, replica_groups=mesh['seqs'=4,'row'=2,'col'=4] {'seqs'}, dimensions={0}, use_global_device_ids=true | all-gather | bytes 737280 | tf_op jit(solution)/shard_map/all_gather | solution.py:215
  (216 shorter events, 106.7 us)
Async XLA Ops:
  7.2 109.4 %all-gather.7.cloned.1.call-start = ((), (), s32[]{:S(2)}) async-start(), calls=%async_computation.16 | async-start | bytes 1622016 | tf_op jit(solution)/shard_map/all_gather | solution.py:203
  9.2 138.4 %all-gather.9.cloned.1.call-start = ((), (), s32[]{:S(2)}) async-start(), calls=%async_computation.17 | async-start | bytes 4055040 | tf_op jit(solution)/shard_map/all_gather | solution.py:203
  13.4 200.1 %all-gather.13.cloned.1.call-start = ((), (), s32[]{:S(2)}) async-start(), calls=%async_computation.19 | async-start | bytes 4866048 | tf_op jit(solution)/shard_map/all_gather | solution.py:203
  14.1 53.9 %copy-start.33 = (f32[768]{0:T(1024)S(1)}, f32[768]{0:T(1024)}, u32[]{:S(2)}) copy-start(f32[768]{0:T(1024)} %param.30) | copy-start | bytes 9220
  14.1 53.9 %copy-start.34 = (f32[192]{0:T(256)S(1)}, f32[192]{0:T(256)}, u32[]{:S(2)}) copy-start(f32[192]{0:T(256)} %param.21) | copy-start | bytes 2308
  14.2 53.9 %copy-start.35 = (f32[192]{0:T(256)S(1)}, f32[192]{0:T(256)}, u32[]{:S(2)}) copy-start(f32[192]{0:T(256)} %param.24) | copy-start | bytes 2308
  14.2 99.9 %copy-start.42 = (s32[8]{0:T(128)S(1)}, s32[8]{0:T(128)}, u32[]{:S(2)}) copy-start(s32[8]{0:T(128)} %param.19) | copy-start | bytes 100
  62.7 64.8 %all-to-all-start.2 = ((bf16[8,192,512]{2,1,0:T(8,128)(2,1)}), bf16[8,192,512]{2,1,0:T(8,128)(2,1)S(1)}, u32[]{:S(2)}, u32[]{:S(2)}) async-start(bf16[8,192,512]{2,1,0:T(8,128)(2,1)} %param.35), calls=%async_computation.2 | async-start | bytes 3145728 | tf_op jit(solution)/shard_map/all_to_all | solution.py:259
  66.3 212.5 %all-gather.11.cloned.1.call-start = ((), (), s32[]{:S(2)}) async-start(), calls=%async_computation.18 | async-start | bytes 4866048 | tf_op jit(solution)/shard_map/all_gather | solution.py:203
  68.0 350.4 %reduce-scatter.21.cloned.1.call-start = ((), (), s32[]{:S(2)}) async-start(), calls=%async_computation.21 | async-start | bytes 1769472 | tf_op jit(solution)/shard_map/reduce_scatter | solution.py:211
  112.7 166.1 %copy-start.31 = (f32[768]{0:T(1024)}, f32[768]{0:T(1024)S(1)}, u32[]{:S(2)}) copy-start(f32[768]{0:T(1024)S(1)} %add.155) | copy-start | bytes 9220
  210.4 123.1 %copy-start.24 = (f32[1024]{0:T(1024)}, f32[1024]{0:T(1024)S(1)}, u32[]{:S(2)}) copy-start(f32[1024]{0:T(1024)S(1)} %get-tuple-element.156) | copy-start | bytes 12292
  210.4 123.1 %copy-start.26 = (f32[1024]{0:T(1024)}, f32[1024]{0:T(1024)S(1)}, u32[]{:S(2)}) copy-start(f32[1024]{0:T(1024)S(1)} %get-tuple-element.157) | copy-start | bytes 12292
  337.4 81.8 %reduce-scatter.37.cloned.1.call-start = ((), (), s32[]{:S(2)}) async-start(), calls=%async_computation.29 | async-start | bytes 5308416
  394.8 26.5 %reduce-scatter.31.cloned.1.call-start = ((), (), s32[]{:S(2)}) async-start(), calls=%async_computation.26 | async-start | bytes 7077888 | tf_op jit(solution)/shard_map/reduce_scatter | solution.py:211
  406.4 31.1 %reduce-scatter.25.cloned.1.call-start = ((), (), s32[]{:S(2)}) async-start(), calls=%async_computation.23 | async-start | bytes 7077888 | tf_op jit(solution)/shard_map/reduce_scatter | solution.py:211
  418.4 48.8 %reduce-scatter.23.cloned.1.call-start = ((), (), s32[]{:S(2)}) async-start(), calls=%async_computation.22 | async-start | bytes 737280 | tf_op jit(solution)/shard_map/reduce_scatter | solution.py:213
  419.1 83.4 %reduce-scatter.39.cloned.1.call-start = ((), (), s32[]{:S(2)}) async-start(), calls=%async_computation.30 | async-start | bytes 2211840
  419.7 123.3 %reduce-scatter.33.cloned.1.call-start = ((), (), s32[]{:S(2)}) async-start(), calls=%async_computation.27 | async-start | bytes 2949120 | tf_op jit(solution)/shard_map/reduce_scatter | solution.py:213
  421.4 162.0 %reduce-scatter.27.cloned.1.call-start = ((), (), s32[]{:S(2)}) async-start(), calls=%async_computation.24 | async-start | bytes 2949120 | tf_op jit(solution)/shard_map/reduce_scatter | solution.py:213
  450.4 42.8 %all-to-all-start.3 = ((bf16[8,192,512]{2,1,0:T(8,128)(2,1)}), bf16[8,192,512]{2,1,0:T(8,128)(2,1)S(1)}, u32[]{:S(2)}, u32[]{:S(2)}) async-start(bf16[8,192,512]{2,1,0:T(8,128)(2,1)} %bitcast.41), calls=%async_computation.3 | async-start | bytes 3145728 | tf_op jit(solution)/shard_map/all_to_all | solution.py:270
  455.4 170.3 %reduce-scatter.41.cloned.1.call-start = ((), (), s32[]{:S(2)}) async-start(), calls=%async_computation.31 | async-start | bytes 245760
  473.2 110.2 %copy-start.6 = (bf16[768,1024]{1,0:T(8,128)(2,1)S(1)}, bf16[768,1024]{1,0:T(8,128)(2,1)}, u32[]{:S(2)}) copy-start(bf16[768,1024]{1,0:T(8,128)(2,1)} %get-tuple-element.24) | copy-start | bytes 4718596
  494.3 89.4 %copy-start.5 = (bf16[768,1024]{1,0:T(8,128)(2,1)S(1)}, bf16[768,1024]{1,0:T(8,128)(2,1)}, u32[]{:S(2)}) copy-start(bf16[768,1024]{1,0:T(8,128)(2,1)} %get-tuple-element.26) | copy-start | bytes 4718596
  494.3 131.3 %all-to-all-start.1 = ((bf16[8,192,512]{2,1,0:T(8,128)(2,1)}), bf16[8,192,512]{2,1,0:T(8,128)(2,1)}, u32[]{:S(2)}, u32[]{:S(2)}) async-start(bf16[8,192,512]{2,1,0:T(8,128)(2,1)} %bitcast.132), calls=%async_computation.1 | async-start | bytes 3145728 | tf_op jit(solution)/shard_map/all_to_all | solution.py:270
  498.8 85.4 %copy-start.30 = (f32[768]{0:T(1024)S(1)}, f32[768]{0:T(1024)}, u32[]{:S(2)}) copy-start(f32[768]{0:T(1024)} %get-tuple-element.114) | copy-start | bytes 9220
  498.8 85.5 %copy-start.29 = (f32[768]{0:T(1024)S(1)}, f32[768]{0:T(1024)}, u32[]{:S(2)}) copy-start(f32[768]{0:T(1024)} %get-tuple-element.117) | copy-start | bytes 9220
  498.8 85.5 %copy-start.28 = (f32[3072]{0:T(1024)S(1)}, f32[3072]{0:T(1024)}, u32[]{:S(2)}) copy-start(f32[3072]{0:T(1024)} %get-tuple-element.162) | copy-start | bytes 36868
  498.8 85.7 %copy-start.21 = (f32[4,192]{1,0:T(4,128)S(1)}, f32[4,192]{1,0:T(4,128)}, u32[]{:S(2)}) copy-start(f32[4,192]{1,0:T(4,128)} %get-tuple-element.122) | copy-start | bytes 9220
  498.8 138.3 %reduce-scatter.19.cloned.1.call-start = ((), (), s32[]{:S(2)}) async-start(), calls=%async_computation.20 | async-start | bytes 737280 | tf_op jit(solution)/shard_map/reduce_scatter | solution.py:214
  504.6 147.0 %reduce-scatter.35.cloned.1.call-start = ((), (), s32[]{:S(2)}) async-start(), calls=%async_computation.28 | async-start | bytes 737280 | tf_op jit(solution)/shard_map/reduce_scatter | solution.py:214
  543.1 131.4 %reduce-scatter.29.cloned.1.call-start = ((), (), s32[]{:S(2)}) async-start(), calls=%async_computation.25 | async-start | bytes 737280 | tf_op jit(solution)/shard_map/reduce_scatter | solution.py:214
  (31 other events, 492.3 us)
Sparse Core Ops, SparseCore 0:
  11.5 61.3 all-gather.6
  76.3 71.2 all-gather.8
  151.1 62.3 all-gather.12
  216.8 61.9 all-gather.10
  337.5 6.7 reduce-scatter.20
  395.0 10.1 reduce-scatter.36
  407.5 13.8 reduce-scatter.30
  423.7 13.8 reduce-scatter.24
  440.4 26.7 reduce-scatter.22
  470.0 32.4 reduce-scatter.38
  505.6 37.3 reduce-scatter.32
  545.9 37.3 reduce-scatter.26
  586.2 19.5 reduce-scatter.40
  608.5 20.3 reduce-scatter.18
  631.1 20.5 reduce-scatter.34
  653.8 20.5 reduce-scatter.28
